TPU v7x, 128 devices: a whole 4x4x4 slice. The times are simulated.
128 devices in a mesh: row: 8 (over y, core), col: 16 (over z, x).
Axes of the slice: x: 4, y: 4, z: 4, core: 2. Of those that a mesh axis runs over, the one named last changes fastest.
Arguments:
- y_blocks: bfloat16 [512, 16, 128, 128], P(('row', 'col')), may hold values from -0.3 to 1.3
- z_blocks: bfloat16 [512, 16, 128, 128], P(('row', 'col')), may hold values from -0.3 to 1.3
- pattern: int32 [512, 16], replicated, may hold values from 0 to 511, as said below
Outputs:
- y_next: bfloat16 [512, 16, 128, 128], P(('row', 'col'))
- z_next: bfloat16 [512, 16, 128, 128], P(('row', 'col'))
Inputs may be any that keep to these rules, and one draw needn't show every extreme that they name: `pattern`: block row i = (16 x + y) * 4 + z belongs to the domain (x, y, z) of a periodic grid of 8 x 16 x 4 domains. It lists 16 distinct block columns, among them i itself; every column is the block row of a domain ((x + a) mod 8, (y + b) mod 16, (z + c) mod 4) with (a, b) one of (0, 0), (1, 0), (-1, 0), (0, 1), (0, -1) and -1 <= c <= 2.
All inputs are finite; a program needn't handle non-finite values.
Results may differ from a plain program's by a relative error of at most 0.0052.
Values may be sent and summed in bfloat16 or wider, within the bound.
A program may use at most 192 MiB of HBM per device.

v0:
```python
import jax
import jax.numpy as jnp
from jax import lax
from jax.sharding import PartitionSpec as P

neighbour_faces = ((-1, 0), (1, 0), (0, -1), (0, 1))
depth_offsets = (-1, 0, 1, 2)


def from_behind(block, axis, distance):
    devices = range(lax.axis_size(axis))
    route = [((i - distance) % len(devices), i) for i in devices]
    return lax.ppermute(block, axis, route)


def domain_start(coord_x, coord_y, layout):
    row_count, col_count, rows_dev = layout
    return (jnp.mod(coord_x, row_count) * col_count + jnp.mod(coord_y, col_count)) * rows_dev


def domain_offsets(columns, base_x, base_y, layout):
    row_count, col_count, rows_dev = layout
    col_x = columns // (col_count * rows_dev)
    col_y = jnp.mod(columns // rows_dev, col_count)
    diff_x = jnp.mod(col_x - base_x, row_count)
    diff_y = jnp.mod(col_y - base_y, col_count)
    return (
        jnp.where(diff_x == row_count - 1, -1, diff_x),
        jnp.where(diff_y == col_count - 1, -1, diff_y),
    )


def factor_faces_full(stacked):
    return [
        from_behind(stacked, "row", 1),
        from_behind(stacked, "row", -1),
        from_behind(stacked, "col", 1),
        from_behind(stacked, "col", -1),
    ]


def update_faces_full(t_blocks):
    return [
        from_behind(t_blocks, "row", 1),
        from_behind(t_blocks, "row", -1),
        from_behind(t_blocks, "col", 1),
        from_behind(t_blocks, "col", -1),
    ]


def sparse_product(factor, extended, own_cols, window_cols, local_index):
    rows_dev = factor.shape[0]
    slot_count = extended.shape[0] // rows_dev
    candidate_count = slot_count * len(depth_offsets)
    candidate_ids = jnp.arange(candidate_count, dtype=jnp.int32)

    def one_row(inputs):
        factor_row, row_columns, row_local, depth = inputs
        starts = [
            slot_index * rows_dev + jnp.mod(depth + offset, rows_dev)
            for slot_index in range(slot_count)
            for offset in depth_offsets
        ]
        candidates = jnp.concatenate(
            [lax.dynamic_slice_in_dim(extended, start, 1, 0) for start in starts], axis=0
        )
        candidate_cols = jnp.concatenate(
            [lax.dynamic_slice_in_dim(window_cols, start, 1, 0) for start in starts], axis=0
        )
        which = row_local // rows_dev * len(depth_offsets) + jnp.mod(
            jnp.mod(row_local, rows_dev) - depth + 1, rows_dev
        )
        row_pick = which[:, None] == candidate_ids[None, :]
        partner = jnp.einsum(
            "kq,qlbc->klbc",
            row_pick.astype(extended.dtype),
            candidates,
            preferred_element_type=jnp.float32,
        ).astype(extended.dtype)
        partner_cols = jnp.sum(
            jnp.where(row_pick[:, :, None], candidate_cols[None, :, :], 0), axis=1
        )
        lane_pick = (partner_cols[:, None, :] == row_columns[None, :, None]).astype(extended.dtype)
        chosen = jnp.einsum(
            "kml,klbc->kmbc", lane_pick, partner, preferred_element_type=jnp.float32
        ).astype(extended.dtype)
        return jnp.einsum("kab,kmbc->mac", factor_row, chosen, preferred_element_type=jnp.float32)

    return lax.map(one_row, (factor, own_cols, local_index, jnp.arange(rows_dev, dtype=jnp.int32)))


def on_device(y_blocks, z_blocks, pattern):
    rows_dev = y_blocks.shape[0]
    layout = (lax.axis_size("row"), lax.axis_size("col"), rows_dev)
    coord_x = lax.axis_index("row")
    coord_y = lax.axis_index("col")
    first_row = domain_start(coord_x, coord_y, layout)
    own_cols = lax.dynamic_slice_in_dim(pattern, first_row, rows_dev, 0)
    near_cols = [
        lax.dynamic_slice_in_dim(
            pattern,
            domain_start(coord_x + offset_pair[0], coord_y + offset_pair[1], layout),
            rows_dev,
            0,
        )
        for offset_pair in neighbour_faces
    ]
    off_x, off_y = domain_offsets(own_cols, coord_x, coord_y, layout)
    slot = jnp.where(
        off_x == -1,
        1,
        jnp.where(off_x == 1, 2, jnp.where(off_y == -1, 3, jnp.where(off_y == 1, 4, 0))),
    )
    local_index = slot * rows_dev + jnp.mod(own_cols, rows_dev)
    stacked = jnp.stack([y_blocks, z_blocks])
    window_cols = jnp.concatenate([own_cols] + near_cols, axis=0)
    received = factor_faces_full(stacked)
    y_ext = jnp.concatenate([y_blocks] + [piece_blocks[0] for piece_blocks in received], axis=0)
    z_ext = jnp.concatenate([z_blocks] + [piece_blocks[1] for piece_blocks in received], axis=0)
    product = sparse_product(z_blocks, y_ext, own_cols, window_cols, local_index)
    diagonal = own_cols == (first_row + jnp.arange(rows_dev, dtype=jnp.int32))[:, None]
    identity = jnp.eye(y_blocks.shape[2], dtype=jnp.float32)
    t_blocks = (
        1.5 * jnp.where(diagonal[:, :, None, None], identity, jnp.float32(0.0)) - 0.5 * product
    ).astype(jnp.bfloat16)
    t_received = update_faces_full(t_blocks)
    t_ext = jnp.concatenate([t_blocks] + t_received, axis=0)
    y_next = sparse_product(y_blocks, t_ext, own_cols, window_cols, local_index).astype(
        jnp.bfloat16
    )
    z_next = sparse_product(t_blocks, z_ext, own_cols, window_cols, local_index).astype(
        jnp.bfloat16
    )
    return (y_next, z_next)


def solution(mesh):
    in_specs = (P(("row", "col"), None, None, None), P(("row", "col"), None, None, None), P())
    out_specs = (P(("row", "col"), None, None, None), P(("row", "col"), None, None, None))
    return jax.shard_map(
        on_device, mesh=mesh, in_specs=in_specs, out_specs=out_specs, check_vma=False
    )
```

profile of v0, /device:TPU:0, one launch (start us, length us, event | category | flops | bytes accessed | tf_op | source)
XLA Modules:
  0.0 1391.2 jit_solution(7784599075909317786)
XLA Ops:
  21.7 33.1 %collective-permute-done = bf16[2,4,16,128,128]{4,3,2,1,0:T(8,128)(2,1)} collective-permute-done((bf16[2,4,16,128,128]{4,3,2,1,0:T(8,128)(2,1)}, bf16[2,4,16,128,128]{4,3,2,1,0:T(8,128)(2,1)}, u32[]{:S(2)}, u32[]{:S(2)}) %collective-permute-start) | collective-permute-done | bytes 4194336 | tf_op jit(solution)/shard_map/ppermute | solution.py:13
  61.0 43.5 %collective-permute-done.2 = bf16[2,4,16,128,128]{4,3,2,1,0:T(8,128)(2,1)} collective-permute-done((bf16[2,4,16,128,128]{4,3,2,1,0:T(8,128)(2,1)}, bf16[2,4,16,128,128]{4,3,2,1,0:T(8,128)(2,1)}, u32[]{:S(2)}, u32[]{:S(2)}) %collective-permute-start.2) | collective-permute-done | bytes 4194336 | tf_op jit(solution)/shard_map/ppermute | solution.py:13
  117.7 417.7 %while.45 = (s32[]{:T(128)}, f32[4,16,128,128]{3,2,1,0:T(8,128)}, s32[4,16]{1,0:T(4,128)S(1)}, s32[4]{0:T(128)S(1)}, s32[20,16]{0,1:T(8,128)S(1)}, /*index=5*/s3...) while((s32[]{:T(128)}, f32[4,16,128,128]{3,2,1,0:T(8,128)}, ...), condition=%wide.region_2.3_spmd.clone.clone, body=%wide.region_0.2_spmd.clone.sunk.clone | while | flops 1375747072 | bytes 104345480 | solution.py:89
  176.1 15.8 %fusion.168 = bf16[16,16,128,128]{3,0,2,1:T(8,128)(2,1)} fusion(bf16[20,16,128,128]{3,2,1,0:T(8,128)(2,1)} %dynamic-slice_dynamic-update-slice_fusion.199, s32[16]{0:T(128)S(1)} %fusion.167), kind=kOutput, calls=%fused_computation.4.clone.1.clone | convolution fusion | flops 167772480 | bytes 18874432 | tf_op jit(solution)/shard_map/while/body/eval_jaxpr/kq,qlbc->klbc/dot_general | solution.py:74
  201.5 12.3 fusion.170
  213.8 12.4 copy.115
  276.7 15.8 %fusion.168 = bf16[16,16,128,128]{3,0,2,1:T(8,128)(2,1)} fusion(bf16[20,16,128,128]{3,2,1,0:T(8,128)(2,1)} %dynamic-slice_dynamic-update-slice_fusion.199, s32[16]{0:T(128)S(1)} %fusion.167), kind=kOutput, calls=%fused_computation.4.clone.1.clone | convolution fusion | flops 167772480 | bytes 18874432 | tf_op jit(solution)/shard_map/while/body/eval_jaxpr/kq,qlbc->klbc/dot_general | solution.py:74
  302.1 12.3 fusion.170
  314.4 12.4 copy.115
  377.3 15.8 %fusion.168 = bf16[16,16,128,128]{3,0,2,1:T(8,128)(2,1)} fusion(bf16[20,16,128,128]{3,2,1,0:T(8,128)(2,1)} %dynamic-slice_dynamic-update-slice_fusion.199, s32[16]{0:T(128)S(1)} %fusion.167), kind=kOutput, calls=%fused_computation.4.clone.1.clone | convolution fusion | flops 167772480 | bytes 18874432 | tf_op jit(solution)/shard_map/while/body/eval_jaxpr/kq,qlbc->klbc/dot_general | solution.py:74
  415.1 12.4 copy.115
  478.0 15.8 %fusion.168 = bf16[16,16,128,128]{3,0,2,1:T(8,128)(2,1)} fusion(bf16[20,16,128,128]{3,2,1,0:T(8,128)(2,1)} %dynamic-slice_dynamic-update-slice_fusion.199, s32[16]{0:T(128)S(1)} %fusion.167), kind=kOutput, calls=%fused_computation.4.clone.1.clone | convolution fusion | flops 167772480 | bytes 18874432 | tf_op jit(solution)/shard_map/while/body/eval_jaxpr/kq,qlbc->klbc/dot_general | solution.py:74
  503.5 12.3 fusion.170
  515.7 12.4 copy.115
  549.1 415.5 %while.47 = (s32[]{:T(128)}, bf16[4,16,128,128]{3,2,1,0:T(8,128)(2,1)}, s32[4,16]{1,0:T(4,128)S(1)}, s32[4]{0:T(128)S(1)}, s32[20,16]{0,1:T(8,128)S(1)}, /*index...) while((s32[]{:T(128)}, ...), condition=%wide.region_8.9_spmd.clone.clone, body=%wide.region_6.8_spmd.clone.sunk.clone | while | flops 1375747072 | bytes 101724040 | solution.py:89
  606.7 15.8 %fusion.190 = bf16[16,16,128,128]{3,0,2,1:T(8,128)(2,1)} fusion(bf16[20,16,128,128]{3,2,1,0:T(8,128)(2,1)} %dynamic-slice_dynamic-update-slice_fusion.239, s32[16]{0:T(128)S(1)} %fusion.189), kind=kOutput, calls=%fused_computation.154.clone.1.clone | convolution fusion | flops 167772480 | bytes 18874432 | tf_op jit(solution)/shard_map/while/body/eval_jaxpr/kq,qlbc->klbc/dot_general | solution.py:74
  644.4 12.4 copy.125
  707.0 15.8 %fusion.190 = bf16[16,16,128,128]{3,0,2,1:T(8,128)(2,1)} fusion(bf16[20,16,128,128]{3,2,1,0:T(8,128)(2,1)} %dynamic-slice_dynamic-update-slice_fusion.239, s32[16]{0:T(128)S(1)} %fusion.189), kind=kOutput, calls=%fused_computation.154.clone.1.clone | convolution fusion | flops 167772480 | bytes 18874432 | tf_op jit(solution)/shard_map/while/body/eval_jaxpr/kq,qlbc->klbc/dot_general | solution.py:74
  744.7 12.4 copy.125
  807.3 15.8 %fusion.190 = bf16[16,16,128,128]{3,0,2,1:T(8,128)(2,1)} fusion(bf16[20,16,128,128]{3,2,1,0:T(8,128)(2,1)} %dynamic-slice_dynamic-update-slice_fusion.239, s32[16]{0:T(128)S(1)} %fusion.189), kind=kOutput, calls=%fused_computation.154.clone.1.clone | convolution fusion | flops 167772480 | bytes 18874432 | tf_op jit(solution)/shard_map/while/body/eval_jaxpr/kq,qlbc->klbc/dot_general | solution.py:74
  845.0 12.4 copy.125
  907.6 15.8 %fusion.190 = bf16[16,16,128,128]{3,0,2,1:T(8,128)(2,1)} fusion(bf16[20,16,128,128]{3,2,1,0:T(8,128)(2,1)} %dynamic-slice_dynamic-update-slice_fusion.239, s32[16]{0:T(128)S(1)} %fusion.189), kind=kOutput, calls=%fused_computation.154.clone.1.clone | convolution fusion | flops 167772480 | bytes 18874432 | tf_op jit(solution)/shard_map/while/body/eval_jaxpr/kq,qlbc->klbc/dot_general | solution.py:74
  945.3 12.4 copy.125
  975.6 415.4 %while.46 = (s32[]{:T(128)}, bf16[4,16,128,128]{3,2,1,0:T(8,128)(2,1)}, s32[4,16]{1,0:T(4,128)S(1)}, s32[4]{0:T(128)S(1)}, s32[20,16]{0,1:T(8,128)S(1)}, /*index...) while((s32[]{:T(128)}, ...), condition=%wide.region_5.6_spmd.clone.clone, body=%wide.region_3.5_spmd.clone.sunk.clone | while | flops 1375747072 | bytes 101724040 | solution.py:89
  1032.9 15.7 %fusion.179 = bf16[16,16,128,128]{3,0,2,1:T(8,128)(2,1)} fusion(bf16[20,16,128,128]{3,2,1,0:T(8,128)(2,1)} %dynamic-slice_dynamic-update-slice_fusion.219, s32[16]{0:T(128)S(1)} %fusion.178), kind=kOutput, calls=%fused_computation.79.clone.1.clone | convolution fusion | flops 167772480 | bytes 18874432 | tf_op jit(solution)/shard_map/while/body/eval_jaxpr/kq,qlbc->klbc/dot_general | solution.py:74
  1070.5 12.5 copy.120
  1133.3 15.7 %fusion.179 = bf16[16,16,128,128]{3,0,2,1:T(8,128)(2,1)} fusion(bf16[20,16,128,128]{3,2,1,0:T(8,128)(2,1)} %dynamic-slice_dynamic-update-slice_fusion.219, s32[16]{0:T(128)S(1)} %fusion.178), kind=kOutput, calls=%fused_computation.79.clone.1.clone | convolution fusion | flops 167772480 | bytes 18874432 | tf_op jit(solution)/shard_map/while/body/eval_jaxpr/kq,qlbc->klbc/dot_general | solution.py:74
  1170.9 12.5 copy.120
  1233.7 15.7 %fusion.179 = bf16[16,16,128,128]{3,0,2,1:T(8,128)(2,1)} fusion(bf16[20,16,128,128]{3,2,1,0:T(8,128)(2,1)} %dynamic-slice_dynamic-update-slice_fusion.219, s32[16]{0:T(128)S(1)} %fusion.178), kind=kOutput, calls=%fused_computation.79.clone.1.clone | convolution fusion | flops 167772480 | bytes 18874432 | tf_op jit(solution)/shard_map/while/body/eval_jaxpr/kq,qlbc->klbc/dot_general | solution.py:74
  1271.3 12.5 copy.120
  1334.1 15.7 %fusion.179 = bf16[16,16,128,128]{3,0,2,1:T(8,128)(2,1)} fusion(bf16[20,16,128,128]{3,2,1,0:T(8,128)(2,1)} %dynamic-slice_dynamic-update-slice_fusion.219, s32[16]{0:T(128)S(1)} %fusion.178), kind=kOutput, calls=%fused_computation.79.clone.1.clone | convolution fusion | flops 167772480 | bytes 18874432 | tf_op jit(solution)/shard_map/while/body/eval_jaxpr/kq,qlbc->klbc/dot_general | solution.py:74
  1371.6 12.5 copy.120
  (450 shorter events, 846.3 us)
Async XLA Ops:
  0.6 18.4 %copy-start.3 = (bf16[4,16,128,128]{3,2,1,0:T(8,128)(2,1)S(1)}, bf16[4,16,128,128]{3,2,1,0:T(8,128)(2,1)}, u32[]{:S(2)}) copy-start(bf16[4,16,128,128]{3,2,1,0:T(8,128)(2,1)} %param.9) | copy-start | bytes 6291460
  0.6 17.1 %copy-start.5 = (s32[512,16]{0,1:T(8,128)S(1)}, s32[512,16]{0,1:T(8,128)}, u32[]{:S(2)}) copy-start(s32[512,16]{0,1:T(8,128)} %param.11) | copy-start | bytes 98308
  5.3 49.5 %collective-permute-start = (bf16[2,4,16,128,128]{4,3,2,1,0:T(8,128)(2,1)}, bf16[2,4,16,128,128]{4,3,2,1,0:T(8,128)(2,1)}, u32[]{:S(2)}, u32[]{:S(2)}) collective-permute-start(bf16[2,4,16,128,128]{4,3,2,1,0:T(8,128)(2,1)} %pad_maximum_fusion), channel_id=1, source_target_pairs={{112,0},{0,16},{16,32},{32,48},{48,64},{64,80},{80,96},{96,112},{1... | collective-permute-start | bytes 12582920 | tf_op jit(solution)/shard_map/ppermute | solution.py:13
  5.4 52.5 %collective-permute-start.1 = (bf16[2,4,16,128,128]{4,3,2,1,0:T(8,128)(2,1)}, bf16[2,4,16,128,128]{4,3,2,1,0:T(8,128)(2,1)}, u32[]{:S(2)}, u32[]{:S(2)}) collective-permute-start(bf16[2,4,16,128,128]{4,3,2,1,0:T(8,128)(2,1)} %pad_maximum_fusion), channel_id=1, source_target_pairs={{16,0},{32,16},{48,32},{64,48},{80,64},{96,80},{112,96},{0,112},{1... | collective-permute-start | bytes 12582920 | tf_op jit(solution)/shard_map/ppermute | solution.py:13
  8.3 96.1 %collective-permute-start.2 = (bf16[2,4,16,128,128]{4,3,2,1,0:T(8,128)(2,1)}, bf16[2,4,16,128,128]{4,3,2,1,0:T(8,128)(2,1)}, u32[]{:S(2)}, u32[]{:S(2)}) collective-permute-start(bf16[2,4,16,128,128]{4,3,2,1,0:T(8,128)(2,1)} %pad_maximum_fusion), channel_id=1, source_target_pairs={{15,0},{0,1},{1,2},{2,3},{3,4},{4,5},{5,6},{6,7},{7,8},{8,9},{9,10... | collective-permute-start | bytes 12582920 | tf_op jit(solution)/shard_map/ppermute | solution.py:13
  9.9 97.6 %collective-permute-start.3 = (bf16[2,4,16,128,128]{4,3,2,1,0:T(8,128)(2,1)}, bf16[2,4,16,128,128]{4,3,2,1,0:T(8,128)(2,1)}, u32[]{:S(2)}, u32[]{:S(2)}) collective-permute-start(bf16[2,4,16,128,128]{4,3,2,1,0:T(8,128)(2,1)} %pad_maximum_fusion), channel_id=1, source_target_pairs={{1,0},{2,1},{3,2},{4,3},{5,4},{6,5},{7,6},{8,7},{9,8},{10,9},{11,1... | collective-permute-start | bytes 12582920 | tf_op jit(solution)/shard_map/ppermute | solution.py:13
  15.1 1.3 copy-start.2
  110.6 3.8 copy-start
  110.6 7.1 copy-start.1
  117.7 417.7 %copy-start.4 = (f32[128,128]{1,0:T(8,128)S(1)}, f32[128,128]{1,0:T(8,128)}, u32[]{:S(2)}) copy-start(f32[128,128]{1,0:T(8,128)} %fusion.83) | copy-start | bytes 196612
  117.7 417.7 %copy-start.6 = (pred[4,16]{1,0:T(4,128)(4,1)S(1)}, pred[4,16]{1,0:T(4,128)(4,1)}, u32[]{:S(2)}) copy-start(pred[4,16]{1,0:T(4,128)(4,1)} %broadcast_compare_fusion) | copy-start | bytes 196
  540.8 423.8 %collective-permute-start.4 = (bf16[4,16,128,128]{3,2,1,0:T(8,128)(2,1)}, bf16[4,16,128,128]{3,2,1,0:T(8,128)(2,1)S(1)}, u32[]{:S(2)}, u32[]{:S(2)}) collective-permute-start(bf16[4,16,128,128]{3,2,1,0:T(8,128)(2,1)} %get-tuple-element.1234), channel_id=1, source_target_pairs={{112,0},{0,16},{16,32},{32,48},{48,64},{64,80},{80,96},{96,112},{1... | collective-permute-start | bytes 6291464 | tf_op jit(solution)/shard_map/ppermute | solution.py:13
  540.8 425.3 %collective-permute-start.5 = (bf16[4,16,128,128]{3,2,1,0:T(8,128)(2,1)}, bf16[4,16,128,128]{3,2,1,0:T(8,128)(2,1)}, u32[]{:S(2)}, u32[]{:S(2)}) collective-permute-start(bf16[4,16,128,128]{3,2,1,0:T(8,128)(2,1)} %get-tuple-element.1234), channel_id=1, source_target_pairs={{16,0},{32,16},{48,32},{64,48},{80,64},{96,80},{112,96},{0,112},{1... | collective-permute-start | bytes 6291464 | tf_op jit(solution)/shard_map/ppermute | solution.py:13
  543.8 425.5 %collective-permute-start.6 = (bf16[4,16,128,128]{3,2,1,0:T(8,128)(2,1)}, bf16[4,16,128,128]{3,2,1,0:T(8,128)(2,1)}, u32[]{:S(2)}, u32[]{:S(2)}) collective-permute-start(bf16[4,16,128,128]{3,2,1,0:T(8,128)(2,1)} %get-tuple-element.1234), channel_id=1, source_target_pairs={{15,0},{0,1},{1,2},{2,3},{3,4},{4,5},{5,6},{6,7},{7,8},{8,9},{9,10... | collective-permute-start | bytes 6291464 | tf_op jit(solution)/shard_map/ppermute | solution.py:13
  543.8 428.7 %collective-permute-start.7 = (bf16[4,16,128,128]{3,2,1,0:T(8,128)(2,1)}, bf16[4,16,128,128]{3,2,1,0:T(8,128)(2,1)}, u32[]{:S(2)}, u32[]{:S(2)}) collective-permute-start(bf16[4,16,128,128]{3,2,1,0:T(8,128)(2,1)} %get-tuple-element.1234), channel_id=1, source_target_pairs={{1,0},{2,1},{3,2},{4,3},{5,4},{6,5},{7,6},{8,7},{9,8},{10,9},{11,1... | collective-permute-start | bytes 6291464 | tf_op jit(solution)/shard_map/ppermute | solution.py:13
where the time goes:
time: 1410 us; the launch traced here: 1390 us
  local copies, waits for them, and re-layouts  774 us (55%)
  matrix products  406 us (29%)
  loops' own time  91.6 us (6%)
  waiting for transfers between devices  76.6 us (5%)
  other arithmetic  25.1 us (2%)
  starting transfers between devices  17.6 us (1%)
    while x228, local copies, waits for them, and re-layouts  433 us
    dot_general x12, matrix products, one_row(): jnp.einsum('kq,qlbc->klbc', row_pick.astype(extended.dtype), candidates,...  189 us
    dot_general x12, local copies, waits for them, and re-layouts, one_row(): jnp.einsum('kml,klbc->kmbc', lane_pick, partner, preferred_element_type=j...  149 us
    dot_general x12, matrix products, one_row(): jnp.einsum('kml,klbc->kmbc', lane_pick, partner, preferred_element_type=j...  147 us
    dot_general x12, local copies, waits for them, and re-layouts, one_row(): jnp.einsum('kq,qlbc->klbc', row_pick.astype(extended.dtype), candidates,...  107 us
    another operation x3, loops' own time, sparse_product(): lax.map(one_row, (factor, own_cols, local_index, jnp.arange(rows_dev, dty...  91.6 us
    ppermute x8, waiting for transfers between devices, from_behind(): return lax.ppermute(block, axis, route)  76.6 us
    dot_general x12, matrix products, one_row(): jnp.einsum('kab,kmbc->mac', factor_row, chosen, preferred_element_type=jn...  69.5 us
  transfers between devices with their start and end apart: 8, of which 2 were waited for; matrix products, arithmetic and copies ran while one was open for 29% of the time, Pallas kernels for 0%

commit v1 on v0

v1 whole, which is shorter than its diff:
```python
import functools

import jax
import jax.numpy as jnp
from jax import lax
from jax.experimental import pallas as pl
from jax.experimental.pallas import tpu as pltpu
from jax.sharding import PartitionSpec as P

MESH = pl.DeviceIdType.MESH
Y_EDGE, Y_DIAG, Z_EDGE, Z_DIAG, T_DIAG = range(5)
SEND_ORDER = (2, 3, 0, 1)


def step_kernel(
    layout,
    y_hbm, z_hbm, pat_hbm,
    y_out, z_out,
    y_raw, z_raw, pat, keep, tab_v, tab,
    y_own, z_own, t_own, got, t_near, y_part, acc, y_acc, z_acc,
    y_dense, z_dense,
    in_sem, send_sem, recv_sem,
):
    row_count, col_count, rows, bs = layout
    lanes = pat.shape[1]
    me_r, me_c = lax.axis_index("row"), lax.axis_index("col")

    def neighbour(d):
        if isinstance(d, int):
            step_r = (-1, 1, 0, 0)[d]
            step_c = (0, 0, -1, 1)[d]
        else:
            step_r = jnp.where(d < 2, 2 * d - 1, 0)
            step_c = jnp.where(d < 2, 0, 2 * d - 5)
        return (
            lax.rem(me_r + step_r + row_count, row_count),
            lax.rem(me_c + step_c + col_count, col_count),
        )

    copies = [
        pltpu.make_async_copy(pat_hbm, pat, in_sem.at[0]),
        pltpu.make_async_copy(y_hbm, y_raw.at[:, 0:lanes], in_sem.at[1]),
        pltpu.make_async_copy(z_hbm, z_raw.at[:, 0:lanes], in_sem.at[2]),
    ]
    for copy in copies:
        copy.start()
    barrier = pltpu.get_barrier_semaphore()
    for d in range(4):
        pl.semaphore_signal(barrier, 1, device_id=neighbour(d), device_id_type=MESH)

    for raw in (y_raw, z_raw):
        for i in range(rows):
            raw[i, lanes] = jnp.zeros((bs, bs), raw.dtype)
    copies[0].wait()
    lane = lax.broadcasted_iota(jnp.int32, (rows, lanes), 1)
    wide = lax.broadcasted_iota(jnp.int32, (rows, 128), 1)

    def base(place):
        return (place[0] * col_count + place[1]) * rows

    def pat_rows(start):
        return pat[pl.ds(pl.multiple_of(start, rows), rows), :]

    bases = [base((me_r, me_c))] + [base(neighbour(d)) for d in range(4)]
    own = pat_rows(bases[0])
    where_own = jnp.zeros((rows, 128), jnp.int32)
    back = jnp.zeros((rows, lanes), jnp.int32)
    for u in range(5):
        for c in range(rows):
            match = own == bases[u] + c
            at = jnp.max(jnp.where(match, lane, -1), axis=1, keepdims=True)
            keep[u, :, c * bs : (c + 1) * bs] = jnp.broadcast_to(at, (rows, bs))
            at = jnp.where(at < 0, lanes, at)
            where_own = jnp.where(wide == u * rows + c, at, where_own)
            back = jnp.where(match, u * rows + c, back)
    for d in range(4):
        near = pat_rows(bases[1 + d])
        for c in range(rows):
            match = near == bases[0] + c
            at = jnp.max(jnp.where(match, lane, -1), axis=1, keepdims=True)
            keep[5 + d, :, c * bs : (c + 1) * bs] = jnp.broadcast_to(at, (rows, bs))
    tab_v[...] = jnp.zeros_like(tab_v)
    tab_v[0:rows, :] = where_own
    tab_v[8 : 8 + rows, 0:lanes] = back
    to_scalar = pltpu.make_async_copy(tab_v, tab, in_sem.at[3])
    to_scalar.start()
    to_scalar.wait()

    def densify(raw, dense, u):
        def one(i, _):
            at_rows = pl.ds(pl.multiple_of(i * bs, bs), bs)
            for c in range(rows):
                dense[u, at_rows, c * bs : (c + 1) * bs] = raw[i, tab[i, u * rows + c]]
            return 0

        lax.fori_loop(0, rows, one, 0)

    def transfer(kind, d, source):
        back_d = d ^ 1 if isinstance(d, int) else d + 1 - 2 * lax.rem(d, 2)
        return pltpu.make_async_remote_copy(
            src_ref=source,
            dst_ref=got.at[kind, back_d],
            send_sem=send_sem.at[kind, d],
            recv_sem=recv_sem.at[kind, back_d],
            device_id=neighbour(d),
            device_id_type=MESH,
        )

    def arrival(kind, d):
        return pltpu.make_async_remote_copy(
            src_ref=got.at[kind, d],
            dst_ref=got.at[kind, d],
            send_sem=send_sem.at[kind, d],
            recv_sem=recv_sem.at[kind, d],
            device_id=neighbour(d),
            device_id_type=MESH,
        )

    sends = []

    def send(kind, d, source):
        copy = transfer(kind, d, source)
        copy.start()
        sends.append(copy)

    copies[1].wait()
    for d in SEND_ORDER:
        densify(y_raw, y_own, 1 + d)
    pl.semaphore_wait(barrier, 4)
    for d in SEND_ORDER:
        send(Y_EDGE, d, y_own.at[1 + d])
    densify(y_raw, y_own, 0)
    for d in SEND_ORDER:
        send(Y_DIAG, d, y_own.at[0])
    copies[2].wait()
    for d in SEND_ORDER:
        densify(z_raw, z_own, 1 + d)
    for d in SEND_ORDER:
        send(Z_EDGE, d, z_own.at[1 + d])
    densify(z_raw, z_own, 0)
    for d in SEND_ORDER:
        send(Z_DIAG, d, z_own.at[0])

    def dot(a, b):
        return jnp.dot(a, b, preferred_element_type=jnp.float32)

    def store_t(target, u, diagonal):
        def one(i, _):
            at_rows = pl.ds(pl.multiple_of(i * bs, bs), bs)
            value = -0.5 * acc[at_rows, :]
            if diagonal:
                r = lax.broadcasted_iota(jnp.int32, value.shape, 0) + i * bs
                s = lax.broadcasted_iota(jnp.int32, value.shape, 1)
                value = jnp.where(r == s, 1.5 + value, value)
            present = jnp.broadcast_to(keep[u, pl.ds(i, 1), :], value.shape) >= 0
            target[at_rows, :] = jnp.where(present, value, 0.0).astype(jnp.bfloat16)
            return 0

        lax.fori_loop(0, rows, one, 0)

    def store_blocks(blocks, u, source):
        def one(i, _):
            at_rows = pl.ds(pl.multiple_of(i * bs, bs), bs)
            for c in range(rows):
                block = source[at_rows, c * bs : (c + 1) * bs]
                blocks[u * rows + c, i] = block.astype(jnp.bfloat16)
            return 0

        lax.fori_loop(0, rows, one, 0)

    acc[...] = dot(z_own[0], y_own[0])

    def add_edge(d, _):
        arrival(Y_EDGE, d).wait_recv()
        acc[...] += dot(z_own[1 + d], got[Y_EDGE, d])
        return 0

    lax.fori_loop(0, 4, add_edge, 0)
    store_t(t_own.at[0], 0, True)
    for d in SEND_ORDER:
        send(T_DIAG, d, t_own.at[0])
    y_acc[...] = dot(y_own[0], t_own[0])
    z_acc[...] = dot(t_own[0], z_own[0])

    def t_edge(d, _):
        acc[...] = dot(z_own[0], y_own[1 + d])
        arrival(Y_DIAG, d).wait_recv()
        acc[...] += dot(z_own[1 + d], got[Y_DIAG, d])
        store_t(t_own.at[1 + d], 1 + d, False)
        y_part[d] = dot(y_own[0], t_own[1 + d])
        return 0

    lax.fori_loop(0, 4, t_edge, 0)

    def z_step(d, _):
        arrival(Z_EDGE, d).wait_recv()
        acc[...] = dot(got[Z_EDGE, d], y_own[0])
        z_acc[...] += dot(t_own[1 + d], got[Z_EDGE, d])
        arrival(Z_DIAG, d).wait_recv()
        acc[...] += dot(got[Z_DIAG, d], got[Y_EDGE, d])
        store_t(t_near, 5 + d, False)
        y_acc[...] += dot(y_own[1 + d], t_near[...])
        acc[...] = dot(t_own[0], z_own[1 + d])
        acc[...] += dot(t_own[1 + d], got[Z_DIAG, d])
        store_blocks(z_dense, 1 + d, acc)
        return 0

    lax.fori_loop(0, 4, z_step, 0)
    store_blocks(z_dense, 0, z_acc)
    store_blocks(y_dense, 0, y_acc)

    def gather(blocks, out):
        def one(i, _):
            for m in range(lanes):
                out[i, m] = blocks[tab[8 + i, m], i]
            return 0

        lax.fori_loop(0, rows, one, 0)

    gather(z_dense, z_out)

    def y_step(d, _):
        arrival(T_DIAG, d).wait_recv()
        acc[...] = y_part[d] + dot(y_own[1 + d], got[T_DIAG, d])
        store_blocks(y_dense, 1 + d, acc)
        return 0

    lax.fori_loop(0, 4, y_step, 0)
    gather(y_dense, y_out)
    for copy in sends:
        copy.wait_send()


def on_device(row_count, col_count, y_blocks, z_blocks, pattern):
    rows, lanes, bs, _ = y_blocks.shape
    size = rows * bs
    bf16, f32 = jnp.bfloat16, jnp.float32
    unit = (size, size)
    out = jax.ShapeDtypeStruct(y_blocks.shape, bf16)
    any_space = pl.BlockSpec(memory_space=pl.ANY)
    vmem = pl.BlockSpec(memory_space=pltpu.VMEM)
    return pl.pallas_call(
        functools.partial(step_kernel, (row_count, col_count, rows, bs)),
        out_shape=(out, out),
        in_specs=[any_space, any_space, any_space],
        out_specs=(vmem, vmem),
        scratch_shapes=[
            pltpu.VMEM((rows, lanes + 1, bs, bs), bf16),
            pltpu.VMEM((rows, lanes + 1, bs, bs), bf16),
            pltpu.VMEM(pattern.shape, jnp.int32),
            pltpu.VMEM((9, rows, size), jnp.int32),
            pltpu.VMEM((16, 128), jnp.int32),
            pltpu.SMEM((16, 128), jnp.int32),
            pltpu.VMEM((5,) + unit, bf16),
            pltpu.VMEM((5,) + unit, bf16),
            pltpu.VMEM((5,) + unit, bf16),
            pltpu.VMEM((5, 4) + unit, bf16),
            pltpu.VMEM(unit, bf16),
            pltpu.VMEM((4,) + unit, f32),
            pltpu.VMEM(unit, f32),
            pltpu.VMEM(unit, f32),
            pltpu.VMEM(unit, f32),
            pltpu.VMEM((5 * rows, rows, bs, bs), bf16),
            pltpu.VMEM((5 * rows, rows, bs, bs), bf16),
            pltpu.SemaphoreType.DMA((4,)),
            pltpu.SemaphoreType.DMA((5, 4)),
            pltpu.SemaphoreType.DMA((5, 4)),
        ],
        compiler_params=pltpu.CompilerParams(
            collective_id=0, has_side_effects=True, vmem_limit_bytes=56 << 20
        ),
    )(y_blocks, z_blocks, pattern)


def solution(mesh):
    spec = P(("row", "col"), None, None, None)
    return jax.shard_map(
        functools.partial(on_device, mesh.shape["row"], mesh.shape["col"]),
        mesh=mesh,
        in_specs=(spec, spec, P()),
        out_specs=(spec, spec),
        check_vma=False,
    )
```

time: 1410 us -> 76.2 us (0.05); the launches traced: 1390 us -> 76 us
  local copies, waits for them, and re-layouts: 774 us -> 6.22 us
  matrix products: 406 us -> 0 us
  loops' own time: 91.6 us -> 0 us
  waiting for transfers between devices: 76.6 us -> 0 us
  Pallas kernels: 0 us -> 69.1 us
  other arithmetic: 25.1 us -> 0 us
  starting transfers between devices: 17.6 us -> 0 us
    while x228 -> x0, local copies, waits for them, and re-layouts: 433 us -> none
    dot_general x36 -> x0, matrix products: 406 us -> none  [the longest x12 189 us: one_row(): jnp.einsum('kq,qlbc->klbc', row_pick.astype(extended.dtype), candidates,...]
    dot_general x24 -> x0, local copies, waits for them, and re-layouts: 256 us -> none  [the longest x12 149 us: one_row(): jnp.einsum('kml,klbc->kmbc', lane_pick, partner, preferred_element_type=j...]
    another operation x3 -> x0, loops' own time: 91.6 us -> none  [sparse_product(): lax.map(one_row, (factor, own_cols, local_index, jnp.arange(rows_dev, dty...]
    ppermute x8 -> x0, waiting for transfers between devices: 76.6 us -> none  [from_behind(): return lax.ppermute(block, axis, route)]
    pallas_call x0 -> x1, Pallas kernels: none -> 69.1 us  [on_device(): pl.pallas_call(functools.partial(step_kernel, (row_count, col_count, rows...]
    concatenate x27 -> x0, local copies, waits for them, and re-layouts: 30.4 us -> none  [the longest x12 22.8 us: one_row(): jnp.concatenate([lax.dynamic_slice_in_dim(extended, start, 1, 0) for star...]
    unnamed x28 -> x5, local copies, waits for them, and re-layouts: 29.2 us -> 6.22 us
  transfers between devices with their start and end apart: 8 -> 0, of which waited for: 2 -> 0; matrix products, arithmetic and copies ran while one was open for 29% -> 0% of each run, Pallas kernels for 0% -> 0%
where the time goes in v1:
time: 76.2 us; the launch traced here: 76 us
  Pallas kernels  69.1 us (91%)
  local copies, waits for them, and re-layouts  6.22 us (8%)
    pallas_call x1, Pallas kernels, on_device(): pl.pallas_call(functools.partial(step_kernel, (row_count, col_count, rows...  69.1 us
    unnamed x5, local copies, waits for them, and re-layouts  6.22 us

profile of v1, /device:TPU:0, one launch (start us, length us, event | category | flops | bytes accessed | tf_op | source)
XLA Modules:
  0.0 76.0 jit_solution(1762463391446647728)
XLA Ops:
  0.6 1.6 %copy.5.pat_hbm = s32[512,16]{1,0:T(8,128)} copy(s32[512,16]{0,1:T(8,128)} %param.5) | data formatting | bytes 65536 | tf_op args[2]
  2.2 69.1 %shard_map.50 = (bf16[4,16,128,128]{3,2,1,0:T(8,128)(2,1)}, bf16[4,16,128,128]{3,2,1,0:T(8,128)(2,1)}) custom-call(bf16[4,16,128,128]{3,2,1,0:T(8,128)(2,1)} %y_hbm.1, bf16[4,16,128,128]{3,2,1,0:T(8,128)(2,1)} %z_hbm.1, s32[512,16]{1,0:T(8,128)} %copy.5.pat_hbm), custom_call_target="tpu_custom_call" | custom-call | tf_op jit(solution)/shard_map/pallas_call | solution.py:242
  71.3 0.0 copy-start
  71.3 3.3 %copy.8 = bf16[4,16,128,128]{3,2,1,0:T(8,128)(2,1)} copy(bf16[4,16,128,128]{3,2,1,0:T(8,128)(2,1)} %get-tuple-element.4) | data formatting | bytes 4194304
  74.6 0.0 copy-done
  74.6 1.3 %copy.9 = bf16[4,16,128,128]{3,2,1,0:T(8,128)(2,1)} copy(bf16[4,16,128,128]{3,2,1,0:T(8,128)(2,1)S(1)} %copy-done) | data formatting | bytes 4194304
Async XLA Ops:
  71.3 3.3 %copy-start = (bf16[4,16,128,128]{3,2,1,0:T(8,128)(2,1)S(1)}, bf16[4,16,128,128]{3,2,1,0:T(8,128)(2,1)}, u32[]{:S(2)}) copy-start(bf16[4,16,128,128]{3,2,1,0:T(8,128)(2,1)} %get-tuple-element.5) | copy-start | bytes 6291460

commit v2 on v1

--- a/solution.py
+++ b/solution.py
@@ -22,7 +22,7 @@
     in_sem, send_sem, recv_sem,
 ):
     row_count, col_count, rows, bs = layout
-    lanes = pat.shape[1]
+    lanes = pat.shape[0]
     me_r, me_c = lax.axis_index("row"), lax.axis_index("col")
 
     def neighbour(d):
@@ -37,6 +37,9 @@
             lax.rem(me_c + step_c + col_count, col_count),
         )
 
+    barrier = pltpu.get_barrier_semaphore()
+    for d in range(4):
+        pl.semaphore_signal(barrier, 1, device_id=neighbour(d), device_id_type=MESH)
     copies = [
         pltpu.make_async_copy(pat_hbm, pat, in_sem.at[0]),
         pltpu.make_async_copy(y_hbm, y_raw.at[:, 0:lanes], in_sem.at[1]),
@@ -44,44 +47,39 @@
     ]
     for copy in copies:
         copy.start()
-    barrier = pltpu.get_barrier_semaphore()
-    for d in range(4):
-        pl.semaphore_signal(barrier, 1, device_id=neighbour(d), device_id_type=MESH)
 
     for raw in (y_raw, z_raw):
         for i in range(rows):
             raw[i, lanes] = jnp.zeros((bs, bs), raw.dtype)
+
+    at_near, at_back = 5 * rows, 9 * rows
     copies[0].wait()
-    lane = lax.broadcasted_iota(jnp.int32, (rows, lanes), 1)
-    wide = lax.broadcasted_iota(jnp.int32, (rows, 128), 1)
-
-    def base(place):
-        return (place[0] * col_count + place[1]) * rows
+    place = lax.broadcasted_iota(jnp.int32, (lanes, 128), 0)
+
+    def base(where):
+        return (where[0] * col_count + where[1]) * rows
 
     def pat_rows(start):
-        return pat[pl.ds(pl.multiple_of(start, rows), rows), :]
+        whole = pat[:, pl.ds(pl.multiple_of(start // 128 * 128, 128), 128)]
+        return pltpu.roll(whole, lax.rem(128 - lax.rem(start, 128), 128), 1)
+
+    def find(columns, column):
+        return jnp.min(jnp.where(columns == column, place, lanes), axis=0, keepdims=True)
 
     bases = [base((me_r, me_c))] + [base(neighbour(d)) for d in range(4)]
     own = pat_rows(bases[0])
-    where_own = jnp.zeros((rows, 128), jnp.int32)
-    back = jnp.zeros((rows, lanes), jnp.int32)
+    back = jnp.zeros((lanes, 128), jnp.int32)
     for u in range(5):
         for c in range(rows):
-            match = own == bases[u] + c
-            at = jnp.max(jnp.where(match, lane, -1), axis=1, keepdims=True)
-            keep[u, :, c * bs : (c + 1) * bs] = jnp.broadcast_to(at, (rows, bs))
-            at = jnp.where(at < 0, lanes, at)
-            where_own = jnp.where(wide == u * rows + c, at, where_own)
-            back = jnp.where(match, u * rows + c, back)
+            q = u * rows + c
+            tab_v[q : q + 1, :] = find(own, bases[u] + c)
+            back = jnp.where(own == bases[u] + c, q, back)
+    tab_v[at_back : at_back + lanes, :] = back
     for d in range(4):
         near = pat_rows(bases[1 + d])
         for c in range(rows):
-            match = near == bases[0] + c
-            at = jnp.max(jnp.where(match, lane, -1), axis=1, keepdims=True)
-            keep[5 + d, :, c * bs : (c + 1) * bs] = jnp.broadcast_to(at, (rows, bs))
-    tab_v[...] = jnp.zeros_like(tab_v)
-    tab_v[0:rows, :] = where_own
-    tab_v[8 : 8 + rows, 0:lanes] = back
+            q = at_near + d * rows + c
+            tab_v[q : q + 1, :] = find(near, bases[0] + c)
     to_scalar = pltpu.make_async_copy(tab_v, tab, in_sem.at[3])
     to_scalar.start()
     to_scalar.wait()
@@ -90,7 +88,7 @@
         def one(i, _):
             at_rows = pl.ds(pl.multiple_of(i * bs, bs), bs)
             for c in range(rows):
-                dense[u, at_rows, c * bs : (c + 1) * bs] = raw[i, tab[i, u * rows + c]]
+                dense[u, at_rows, c * bs : (c + 1) * bs] = raw[i, tab[u * rows + c, i]]
             return 0
 
         lax.fori_loop(0, rows, one, 0)
@@ -124,10 +122,13 @@
         sends.append(copy)
 
     copies[1].wait()
-    for d in SEND_ORDER:
+    densify(y_raw, y_own, 3)
+    pl.semaphore_wait(barrier, 4)
+    send(Y_EDGE, 2, y_own.at[3])
+    densify(y_raw, y_own, 4)
+    send(Y_EDGE, 3, y_own.at[4])
+    for d in (0, 1):
         densify(y_raw, y_own, 1 + d)
-    pl.semaphore_wait(barrier, 4)
-    for d in SEND_ORDER:
         send(Y_EDGE, d, y_own.at[1 + d])
     densify(y_raw, y_own, 0)
     for d in SEND_ORDER:
@@ -135,11 +136,17 @@
     copies[2].wait()
     for d in SEND_ORDER:
         densify(z_raw, z_own, 1 + d)
-    for d in SEND_ORDER:
         send(Z_EDGE, d, z_own.at[1 + d])
     densify(z_raw, z_own, 0)
     for d in SEND_ORDER:
         send(Z_DIAG, d, z_own.at[0])
+
+    for u in range(9):
+        for c in range(rows):
+            for i in range(rows):
+                keep[u, i : i + 1, c * bs : (c + 1) * bs] = jnp.full(
+                    (1, bs), tab[u * rows + c, i], jnp.int32
+                )
 
     def dot(a, b):
         return jnp.dot(a, b, preferred_element_type=jnp.float32)
@@ -152,7 +159,7 @@
                 r = lax.broadcasted_iota(jnp.int32, value.shape, 0) + i * bs
                 s = lax.broadcasted_iota(jnp.int32, value.shape, 1)
                 value = jnp.where(r == s, 1.5 + value, value)
-            present = jnp.broadcast_to(keep[u, pl.ds(i, 1), :], value.shape) >= 0
+            present = jnp.broadcast_to(keep[u, pl.ds(i, 1), :], value.shape) < lanes
             target[at_rows, :] = jnp.where(present, value, 0.0).astype(jnp.bfloat16)
             return 0
 
@@ -212,7 +219,7 @@
     def gather(blocks, out):
         def one(i, _):
             for m in range(lanes):
-                out[i, m] = blocks[tab[8 + i, m], i]
+                out[i, m] = blocks[tab[at_back + m, i], i]
             return 0
 
         lax.fori_loop(0, rows, one, 0)
@@ -231,26 +238,38 @@
         copy.wait_send()
 
 
+def write_kernel(y_vmem, z_vmem, y_out, z_out, sem):
+    copies = []
+    for n, (source, target) in enumerate(((z_vmem, z_out), (y_vmem, y_out))):
+        for i in range(source.shape[0]):
+            copies.append(pltpu.make_async_copy(source.at[i], target.at[i], sem.at[n, i]))
+    for copy in copies:
+        copy.start()
+    for copy in copies:
+        copy.wait()
+
+
 def on_device(row_count, col_count, y_blocks, z_blocks, pattern):
     rows, lanes, bs, _ = y_blocks.shape
     size = rows * bs
     bf16, f32 = jnp.bfloat16, jnp.float32
     unit = (size, size)
+    held = pltpu.VMEM(y_blocks.shape, bf16)
     out = jax.ShapeDtypeStruct(y_blocks.shape, bf16)
     any_space = pl.BlockSpec(memory_space=pl.ANY)
     vmem = pl.BlockSpec(memory_space=pltpu.VMEM)
-    return pl.pallas_call(
+    y_vmem, z_vmem = pl.pallas_call(
         functools.partial(step_kernel, (row_count, col_count, rows, bs)),
-        out_shape=(out, out),
+        out_shape=(held, held),
         in_specs=[any_space, any_space, any_space],
         out_specs=(vmem, vmem),
         scratch_shapes=[
             pltpu.VMEM((rows, lanes + 1, bs, bs), bf16),
             pltpu.VMEM((rows, lanes + 1, bs, bs), bf16),
-            pltpu.VMEM(pattern.shape, jnp.int32),
+            pltpu.VMEM((lanes, pattern.shape[0]), jnp.int32),
             pltpu.VMEM((9, rows, size), jnp.int32),
-            pltpu.VMEM((16, 128), jnp.int32),
-            pltpu.SMEM((16, 128), jnp.int32),
+            pltpu.VMEM((9 * rows + lanes, 128), jnp.int32),
+            pltpu.SMEM((9 * rows + lanes, 128), jnp.int32),
             pltpu.VMEM((5,) + unit, bf16),
             pltpu.VMEM((5,) + unit, bf16),
             pltpu.VMEM((5,) + unit, bf16),
@@ -267,9 +286,20 @@
             pltpu.SemaphoreType.DMA((5, 4)),
         ],
         compiler_params=pltpu.CompilerParams(
-            collective_id=0, has_side_effects=True, vmem_limit_bytes=56 << 20
+            collective_id=0, has_side_effects=True, vmem_limit_bytes=48 << 20
         ),
-    )(y_blocks, z_blocks, pattern)
+    )(y_blocks, z_blocks, pltpu.with_memory_space_constraint(pattern.T, pltpu.HBM))
+    return pl.pallas_call(
+        write_kernel,
+        out_shape=(out, out),
+        in_specs=[vmem, vmem],
+        out_specs=(any_space, any_space),
+        scratch_shapes=[pltpu.SemaphoreType.DMA((2, rows))],
+        compiler_params=pltpu.CompilerParams(vmem_limit_bytes=1 << 20),
+    )(
+        pltpu.with_memory_space_constraint(y_vmem, pltpu.VMEM),
+        pltpu.with_memory_space_constraint(z_vmem, pltpu.VMEM),
+    )
 
 
 def solution(mesh):

time: 76.2 us -> 69.9 us (0.917)
  local copies, waits for them, and re-layouts: 6.22 us -> 0 us
    unnamed x5 -> x0, local copies, waits for them, and re-layouts: 6.22 us -> none
    pallas_call x0 -> x1, Pallas kernels: none -> 2.07 us  [on_device(): pl.pallas_call(write_kernel, out_shape=(out, out), in_specs=[vmem, vmem],...]
    pallas_call x1, Pallas kernels: 69.1 us -> 67.1 us  [on_device(): pl.pallas_call(functools.partial(step_kernel, (row_count, col_count, rows...]
where the time goes in v2:
time: 69.9 us; the launch traced here: 69.8 us
  Pallas kernels  69.2 us (99%)
    pallas_call x1, Pallas kernels, on_device(): pl.pallas_call(functools.partial(step_kernel, (row_count, col_count, rows...  67.1 us
    pallas_call x1, Pallas kernels, on_device(): pl.pallas_call(write_kernel, out_shape=(out, out), in_specs=[vmem, vmem],...  2.07 us

profile of v2, /device:TPU:0, one launch (start us, length us, event | category | flops | bytes accessed | tf_op | source)
XLA Modules:
  0.0 69.8 jit_solution(17825578921349279687)
XLA Ops:
  0.6 67.1 %shard_map.50 = (bf16[4,16,128,128]{3,2,1,0:T(8,128)(2,1)S(1)}, bf16[4,16,128,128]{3,2,1,0:T(8,128)(2,1)S(1)}) custom-call(bf16[4,16,128,128]{3,2,1,0:T(8,128)(2,1)} %y_hbm.1, bf16[4,16,128,128]{3,2,1,0:T(8,128)(2,1)} %z_hbm.1, s32[16,512]{1,0:T(8,128)} %bitcast.1), custom_call_target="tpu_custom_call" | custom-call | tf_op jit(solution)/shard_map/pallas_call | solution.py:261
  67.7 2.1 %shard_map.51 = (bf16[4,16,128,128]{3,2,1,0:T(8,128)(2,1)}, bf16[4,16,128,128]{3,2,1,0:T(8,128)(2,1)}) custom-call(bf16[4,16,128,128]{3,2,1,0:T(8,128)(2,1)S(1)} %get-tuple-element.4.y_vmem, bf16[4,16,128,128]{3,2,1,0:T(8,128)(2,1)S(1)} %get-tuple-element.5.z_vmem), custom_call_target="tpu_custom_call" | custom-call | tf_op jit(solution)/shard_map/pallas_call | solution.py:292

commit v3 on v2

--- a/solution.py
+++ b/solution.py
@@ -9,6 +9,7 @@
 
 MESH = pl.DeviceIdType.MESH
 Y_EDGE, Y_DIAG, Z_EDGE, Z_DIAG, T_DIAG = range(5)
+T_PARTS = 2
 SEND_ORDER = (2, 3, 0, 1)
 
 
@@ -93,21 +94,29 @@
 
         lax.fori_loop(0, rows, one, 0)
 
+    size = rows * bs
+    width = size // T_PARTS
+
+    def target(kind, d):
+        if kind < T_DIAG:
+            return got.at[kind, d]
+        n = kind - T_DIAG
+        return got.at[T_DIAG, d, :, n * width : (n + 1) * width]
+
     def transfer(kind, d, source):
-        back_d = d ^ 1 if isinstance(d, int) else d + 1 - 2 * lax.rem(d, 2)
         return pltpu.make_async_remote_copy(
             src_ref=source,
-            dst_ref=got.at[kind, back_d],
+            dst_ref=target(kind, d ^ 1),
             send_sem=send_sem.at[kind, d],
-            recv_sem=recv_sem.at[kind, back_d],
+            recv_sem=recv_sem.at[kind, d ^ 1],
             device_id=neighbour(d),
             device_id_type=MESH,
         )
 
     def arrival(kind, d):
         return pltpu.make_async_remote_copy(
-            src_ref=got.at[kind, d],
-            dst_ref=got.at[kind, d],
+            src_ref=target(kind, d),
+            dst_ref=target(kind, d),
             send_sem=send_sem.at[kind, d],
             recv_sem=recv_sem.at[kind, d],
             device_id=neighbour(d),
@@ -184,8 +193,9 @@
 
     lax.fori_loop(0, 4, add_edge, 0)
     store_t(t_own.at[0], 0, True)
-    for d in SEND_ORDER:
-        send(T_DIAG, d, t_own.at[0])
+    for n in range(T_PARTS):
+        for d in SEND_ORDER:
+            send(T_DIAG + n, d, t_own.at[0, :, n * width : (n + 1) * width])
     y_acc[...] = dot(y_own[0], t_own[0])
     z_acc[...] = dot(t_own[0], z_own[0])
 
@@ -226,13 +236,20 @@
 
     gather(z_dense, z_out)
 
-    def y_step(d, _):
-        arrival(T_DIAG, d).wait_recv()
-        acc[...] = y_part[d] + dot(y_own[1 + d], got[T_DIAG, d])
-        store_blocks(y_dense, 1 + d, acc)
-        return 0
-
-    lax.fori_loop(0, 4, y_step, 0)
+    for n in range(T_PARTS):
+        cols = slice(n * width, (n + 1) * width)
+
+        def y_step(d, _):
+            arrival(T_DIAG + n, d).wait_recv()
+            part = dot(y_own[1 + d], got[T_DIAG, d, :, cols]) + y_part[d, :, cols]
+            part = part.astype(jnp.bfloat16)
+            for i in range(rows):
+                for c in range(width // bs):
+                    q = (1 + d) * rows + n * (width // bs) + c
+                    y_dense[q, i] = part[i * bs : (i + 1) * bs, c * bs : (c + 1) * bs]
+            return 0
+
+        lax.fori_loop(0, 4, y_step, 0)
     gather(y_dense, y_out)
     for copy in sends:
         copy.wait_send()
@@ -241,8 +258,7 @@
 def write_kernel(y_vmem, z_vmem, y_out, z_out, sem):
     copies = []
     for n, (source, target) in enumerate(((z_vmem, z_out), (y_vmem, y_out))):
-        for i in range(source.shape[0]):
-            copies.append(pltpu.make_async_copy(source.at[i], target.at[i], sem.at[n, i]))
+        copies.append(pltpu.make_async_copy(source, target, sem.at[n, 0]))
     for copy in copies:
         copy.start()
     for copy in copies:
@@ -282,8 +298,8 @@
             pltpu.VMEM((5 * rows, rows, bs, bs), bf16),
             pltpu.VMEM((5 * rows, rows, bs, bs), bf16),
             pltpu.SemaphoreType.DMA((4,)),
-            pltpu.SemaphoreType.DMA((5, 4)),
-            pltpu.SemaphoreType.DMA((5, 4)),
+            pltpu.SemaphoreType.DMA((4 + T_PARTS, 4)),
+            pltpu.SemaphoreType.DMA((4 + T_PARTS, 4)),
         ],
         compiler_params=pltpu.CompilerParams(
             collective_id=0, has_side_effects=True, vmem_limit_bytes=48 << 20

time: 69.9 us -> 69.5 us (level)
  no operation moved by 1% of the time
where the time goes in v3:
time: 69.5 us; the launch traced here: 69.4 us
  Pallas kernels  68.8 us (99%)
    pallas_call x1, Pallas kernels, on_device(): pl.pallas_call(functools.partial(step_kernel, (row_count, col_count, rows...  66.7 us
    pallas_call x1, Pallas kernels, on_device(): pl.pallas_call(write_kernel, out_shape=(out, out), in_specs=[vmem, vmem],...  2.08 us

profile of v3, /device:TPU:0, one launch (start us, length us, event | category | flops | bytes accessed | tf_op | source)
XLA Modules:
  0.0 69.4 jit_solution(3506307236925441768)
XLA Ops:
  0.6 66.7 %shard_map.50 = (bf16[4,16,128,128]{3,2,1,0:T(8,128)(2,1)S(1)}, bf16[4,16,128,128]{3,2,1,0:T(8,128)(2,1)S(1)}) custom-call(bf16[4,16,128,128]{3,2,1,0:T(8,128)(2,1)} %y_hbm.1, bf16[4,16,128,128]{3,2,1,0:T(8,128)(2,1)} %z_hbm.1, s32[16,512]{1,0:T(8,128)} %bitcast.1), custom_call_target="tpu_custom_call" | custom-call | tf_op jit(solution)/shard_map/pallas_call | solution.py:277
  67.4 2.1 %shard_map.51 = (bf16[4,16,128,128]{3,2,1,0:T(8,128)(2,1)}, bf16[4,16,128,128]{3,2,1,0:T(8,128)(2,1)}) custom-call(bf16[4,16,128,128]{3,2,1,0:T(8,128)(2,1)S(1)} %get-tuple-element.4.y_vmem, bf16[4,16,128,128]{3,2,1,0:T(8,128)(2,1)S(1)} %get-tuple-element.5.z_vmem), custom_call_target="tpu_custom_call" | custom-call | tf_op jit(solution)/shard_map/pallas_call | solution.py:308

commit v4 on v3

--- a/solution.py
+++ b/solution.py
@@ -9,7 +9,9 @@
 
 MESH = pl.DeviceIdType.MESH
 Y_EDGE, Y_DIAG, Z_EDGE, Z_DIAG, T_DIAG = range(5)
-T_PARTS = 2
+T_PARTS = (2, 1, 1)
+T_KINDS = len(T_PARTS) + 1
+LAP = 4
 SEND_ORDER = (2, 3, 0, 1)
 
 
@@ -20,7 +22,7 @@
     y_raw, z_raw, pat, keep, tab_v, tab,
     y_own, z_own, t_own, got, t_near, y_part, acc, y_acc, z_acc,
     y_dense, z_dense,
-    in_sem, send_sem, recv_sem,
+    relay_buf, in_sem, send_sem, recv_sem, relay_sem, entered,
 ):
     row_count, col_count, rows, bs = layout
     lanes = pat.shape[0]
@@ -39,8 +41,20 @@
         )
 
     barrier = pltpu.get_barrier_semaphore()
-    for d in range(4):
-        pl.semaphore_signal(barrier, 1, device_id=neighbour(d), device_id_type=MESH)
+    detours = (me_c == LAP - 1, me_c == col_count - 1)
+    detours = (detours[1], detours[0] | detours[1])
+    relays = (me_c == LAP - 1, (me_c == LAP - 1) | (me_c == 2 * LAP - 1))
+    ends = (me_c == 0) | (me_c == LAP)
+    relay_place = (me_r, lax.rem(me_c + LAP, col_count))
+    end_place = (me_r, lax.rem(me_c + col_count + 1 - LAP, col_count))
+
+    def greet(place):
+        pl.semaphore_signal(barrier, 1, device_id=place, device_id_type=MESH)
+
+    for d in (0, 1, 2):
+        greet(neighbour(d))
+    pl.when(relays[1])(lambda: greet((me_r, lax.rem(me_c + col_count - LAP, col_count))))
+    pl.when(ends)(lambda: greet((me_r, lax.rem(me_c + LAP - 1, col_count))))
     copies = [
         pltpu.make_async_copy(pat_hbm, pat, in_sem.at[0]),
         pltpu.make_async_copy(y_hbm, y_raw.at[:, 0:lanes], in_sem.at[1]),
@@ -83,6 +97,8 @@
             tab_v[q : q + 1, :] = find(near, bases[0] + c)
     to_scalar = pltpu.make_async_copy(tab_v, tab, in_sem.at[3])
     to_scalar.start()
+    pl.semaphore_wait(barrier, 3 + jnp.where(detours[1], 1, 0) + jnp.where(relays[1], 1, 0))
+    pl.semaphore_signal(entered, 1, device_id=neighbour(3), device_id_type=MESH)
     to_scalar.wait()
 
     def densify(raw, dense, u):
@@ -95,13 +111,18 @@
         lax.fori_loop(0, rows, one, 0)
 
     size = rows * bs
-    width = size // T_PARTS
+    part_cols = []
+    for n, width in enumerate(T_PARTS):
+        start = sum(T_PARTS[:n]) * bs
+        part_cols.append(slice(start, start + width * bs))
+    pieces = [(slice(0, size), cols) for cols in part_cols[:-1]]
+    pieces += [(slice(0, size // 2), part_cols[-1]), (slice(size // 2, size), part_cols[-1])]
 
     def target(kind, d):
         if kind < T_DIAG:
             return got.at[kind, d]
-        n = kind - T_DIAG
-        return got.at[T_DIAG, d, :, n * width : (n + 1) * width]
+        at_rows, cols = pieces[kind - T_DIAG]
+        return got.at[T_DIAG, d, at_rows, cols]
 
     def transfer(kind, d, source):
         return pltpu.make_async_remote_copy(
@@ -131,17 +152,18 @@
         sends.append(copy)
 
     copies[1].wait()
-    densify(y_raw, y_own, 3)
-    pl.semaphore_wait(barrier, 4)
-    send(Y_EDGE, 2, y_own.at[3])
     densify(y_raw, y_own, 4)
     send(Y_EDGE, 3, y_own.at[4])
     for d in (0, 1):
         densify(y_raw, y_own, 1 + d)
         send(Y_EDGE, d, y_own.at[1 + d])
     densify(y_raw, y_own, 0)
-    for d in SEND_ORDER:
+    densify(y_raw, y_own, 3)
+    for d in (3, 0, 1):
         send(Y_DIAG, d, y_own.at[0])
+    pl.semaphore_wait(entered, 1)
+    send(Y_EDGE, 2, y_own.at[3])
+    send(Y_DIAG, 2, y_own.at[0])
     copies[2].wait()
     for d in SEND_ORDER:
         densify(z_raw, z_own, 1 + d)
@@ -193,9 +215,40 @@
 
     lax.fori_loop(0, 4, add_edge, 0)
     store_t(t_own.at[0], 0, True)
-    for n in range(T_PARTS):
+    hops, forwards = [], []
+    for p in range(2):
+        kind = T_DIAG + T_KINDS - 2 + p
+        hops.append(
+            pltpu.make_async_remote_copy(
+                src_ref=t_own.at[0, pieces[kind - T_DIAG][0], pieces[kind - T_DIAG][1]],
+                dst_ref=relay_buf.at[p],
+                send_sem=send_sem.at[kind, 3],
+                recv_sem=relay_sem.at[p, 0],
+                device_id=relay_place,
+                device_id_type=MESH,
+            )
+        )
+        forwards.append(
+            pltpu.make_async_remote_copy(
+                src_ref=relay_buf.at[p],
+                dst_ref=target(kind, 2),
+                send_sem=relay_sem.at[p, 1],
+                recv_sem=recv_sem.at[kind, 2],
+                device_id=end_place,
+                device_id_type=MESH,
+            )
+        )
+    for n in range(T_KINDS):
+        p = n - (T_KINDS - 2)
         for d in SEND_ORDER:
-            send(T_DIAG + n, d, t_own.at[0, :, n * width : (n + 1) * width])
+            source = t_own.at[0, pieces[n][0], pieces[n][1]]
+            if p >= 0 and d == 3:
+                direct = transfer(T_DIAG + n, d, source)
+                pl.when(detours[p])(hops[p].start)
+                pl.when(jnp.logical_not(detours[p]))(direct.start)
+                sends.append(direct)
+            else:
+                send(T_DIAG + n, d, source)
     y_acc[...] = dot(y_own[0], t_own[0])
     z_acc[...] = dot(t_own[0], z_own[0])
 
@@ -208,6 +261,13 @@
         return 0
 
     lax.fori_loop(0, 4, t_edge, 0)
+
+    def pass_on(p):
+        hops[p].wait_recv()
+        forwards[p].start()
+
+    for p in range(2):
+        pl.when(relays[p])(functools.partial(pass_on, p))
 
     def z_step(d, _):
         arrival(Z_EDGE, d).wait_recv()
@@ -236,16 +296,18 @@
 
     gather(z_dense, z_out)
 
-    for n in range(T_PARTS):
-        cols = slice(n * width, (n + 1) * width)
+    for n, width in enumerate(T_PARTS):
+        cols = part_cols[n]
 
         def y_step(d, _):
             arrival(T_DIAG + n, d).wait_recv()
+            if n == len(T_PARTS) - 1:
+                arrival(T_DIAG + n + 1, d).wait_recv()
             part = dot(y_own[1 + d], got[T_DIAG, d, :, cols]) + y_part[d, :, cols]
             part = part.astype(jnp.bfloat16)
             for i in range(rows):
-                for c in range(width // bs):
-                    q = (1 + d) * rows + n * (width // bs) + c
+                for c in range(width):
+                    q = (1 + d) * rows + sum(T_PARTS[:n]) + c
                     y_dense[q, i] = part[i * bs : (i + 1) * bs, c * bs : (c + 1) * bs]
             return 0
 
@@ -253,6 +315,8 @@
     gather(y_dense, y_out)
     for copy in sends:
         copy.wait_send()
+    for p in range(2):
+        pl.when(relays[p])(forwards[p].wait_send)
 
 
 def write_kernel(y_vmem, z_vmem, y_out, z_out, sem):
@@ -297,9 +361,12 @@
             pltpu.VMEM(unit, f32),
             pltpu.VMEM((5 * rows, rows, bs, bs), bf16),
             pltpu.VMEM((5 * rows, rows, bs, bs), bf16),
+            pltpu.VMEM((2, size // 2, T_PARTS[-1] * bs), bf16),
             pltpu.SemaphoreType.DMA((4,)),
-            pltpu.SemaphoreType.DMA((4 + T_PARTS, 4)),
-            pltpu.SemaphoreType.DMA((4 + T_PARTS, 4)),
+            pltpu.SemaphoreType.DMA((4 + T_KINDS, 4)),
+            pltpu.SemaphoreType.DMA((4 + T_KINDS, 4)),
+            pltpu.SemaphoreType.DMA((2, 2)),
+            pltpu.SemaphoreType.REGULAR,
         ],
         compiler_params=pltpu.CompilerParams(
             collective_id=0, has_side_effects=True, vmem_limit_bytes=48 << 20

time: 69.5 us -> 68 us (0.978)
  Pallas kernels: 68.8 us -> 67.2 us
    pallas_call x1, Pallas kernels: 66.7 us -> 65.2 us  [on_device(): pl.pallas_call(functools.partial(step_kernel, (row_count, col_count, rows...]
where the time goes in v4:
time: 68 us; the launch traced here: 67.9 us
  Pallas kernels  67.2 us (99%)
    pallas_call x1, Pallas kernels, on_device(): pl.pallas_call(functools.partial(step_kernel, (row_count, col_count, rows...  65.2 us
    pallas_call x1, Pallas kernels, on_device(): pl.pallas_call(write_kernel, out_shape=(out, out), in_specs=[vmem, vmem],...  2.08 us

profile of v4, /device:TPU:0, one launch (start us, length us, event | category | flops | bytes accessed | tf_op | source)
XLA Modules:
  0.0 67.9 jit_solution(12307332633742257039)
XLA Ops:
  0.6 65.2 %shard_map.50 = (bf16[4,16,128,128]{3,2,1,0:T(8,128)(2,1)S(1)}, bf16[4,16,128,128]{3,2,1,0:T(8,128)(2,1)S(1)}) custom-call(bf16[4,16,128,128]{3,2,1,0:T(8,128)(2,1)} %y_hbm.1, bf16[4,16,128,128]{3,2,1,0:T(8,128)(2,1)} %z_hbm.1, s32[16,512]{1,0:T(8,128)} %bitcast.1), custom_call_target="tpu_custom_call" | custom-call | tf_op jit(solution)/shard_map/pallas_call | solution.py:341
  65.8 2.1 %shard_map.51 = (bf16[4,16,128,128]{3,2,1,0:T(8,128)(2,1)}, bf16[4,16,128,128]{3,2,1,0:T(8,128)(2,1)}) custom-call(bf16[4,16,128,128]{3,2,1,0:T(8,128)(2,1)S(1)} %get-tuple-element.4.y_vmem, bf16[4,16,128,128]{3,2,1,0:T(8,128)(2,1)S(1)} %get-tuple-element.5.z_vmem), custom_call_target="tpu_custom_call" | custom-call | tf_op jit(solution)/shard_map/pallas_call | solution.py:375

commit v5 on v4

--- a/solution.py
+++ b/solution.py
@@ -12,7 +12,7 @@
 T_PARTS = (2, 1, 1)
 T_KINDS = len(T_PARTS) + 1
 LAP = 4
-SEND_ORDER = (2, 3, 0, 1)
+SEND_ORDER = (3, 2, 0, 1)
 
 
 def step_kernel(

time: 68 us -> 68 us (level)
  no operation moved by 1% of the time
where the time goes in v5:
time: 68 us; the launch traced here: 67.9 us
  Pallas kernels  67.2 us (99%)
    pallas_call x1, Pallas kernels, on_device(): pl.pallas_call(functools.partial(step_kernel, (row_count, col_count, rows...  65.2 us
    pallas_call x1, Pallas kernels, on_device(): pl.pallas_call(write_kernel, out_shape=(out, out), in_specs=[vmem, vmem],...  2.08 us

profile of v5, /device:TPU:0, one launch (start us, length us, event | category | flops | bytes accessed | tf_op | source)
XLA Modules:
  0.0 67.9 jit_solution(7667199737053262135)
XLA Ops:
  0.6 65.2 %shard_map.50 = (bf16[4,16,128,128]{3,2,1,0:T(8,128)(2,1)S(1)}, bf16[4,16,128,128]{3,2,1,0:T(8,128)(2,1)S(1)}) custom-call(bf16[4,16,128,128]{3,2,1,0:T(8,128)(2,1)} %y_hbm.1, bf16[4,16,128,128]{3,2,1,0:T(8,128)(2,1)} %z_hbm.1, s32[16,512]{1,0:T(8,128)} %bitcast.1), custom_call_target="tpu_custom_call" | custom-call | tf_op jit(solution)/shard_map/pallas_call | solution.py:341
  65.8 2.1 %shard_map.51 = (bf16[4,16,128,128]{3,2,1,0:T(8,128)(2,1)}, bf16[4,16,128,128]{3,2,1,0:T(8,128)(2,1)}) custom-call(bf16[4,16,128,128]{3,2,1,0:T(8,128)(2,1)S(1)} %get-tuple-element.4.y_vmem, bf16[4,16,128,128]{3,2,1,0:T(8,128)(2,1)S(1)} %get-tuple-element.5.z_vmem), custom_call_target="tpu_custom_call" | custom-call | tf_op jit(solution)/shard_map/pallas_call | solution.py:375
